TPU v7x, 256 devices: a whole 4x4x8 slice. The times are simulated.
256 devices in a mesh: grp: 64 (over z, y, core), head: 4 (over x).
Axes of the slice: x: 4, y: 4, z: 8, core: 2. Of those that a mesh axis runs over, the one named last changes fastest.
Arguments:
- arriving_hiddens: bfloat16 [512, 4, 2048], P('grp', None, 'head'), may hold values from -6 to 6
- occupied_slot_totals: int32 [512], P('grp'), may hold values from 1 to 4
- former_indices: int32 [512], P('grp'), may hold values from 0 to 511, as said below
- reconstruct_marks: int32 [512], P('grp'), may hold values from 0 to 1, as said below
- retained_hiddens: bfloat16 [512, 32, 2048], P('grp', None, 'head'), may hold values from -6 to 6
- carried_memory_matrices: float32 [512, 16, 64, 64], P('grp', 'head'), may hold values from -12 to 12
- lagged_previous_entries: float32 [512, 2, 2048], P('grp', None, 'head'), may hold values from -6 to 6
- pre_attention_scaling: float32 [2048], replicated, may hold values from 0.5 to 1.5
- pre_feedforward_scaling: float32 [2048], replicated, may hold values from 0.5 to 1.5
- lag_blend_fractions: float32 [5, 2048], replicated, may hold values from 0 to 1
- acceptance_projection: bfloat16 [2048, 1024], P(None, 'head'), may hold values from -0.125 to 0.125
- address_projection: bfloat16 [2048, 1024], P(None, 'head'), may hold values from -0.125 to 0.125
- content_projection: bfloat16 [2048, 1024], P(None, 'head'), may hold values from -0.125 to 0.125
- fading_lowrank_left: bfloat16 [2048, 64], replicated, may hold values from -0.125 to 0.125
- fading_lowrank_right: bfloat16 [64, 1024], P(None, 'head'), may hold values from -0.75 to 0.75
- fading_baseline_entries: float32 [1024], P('head'), may hold values from -6 to 1
- present_item_reward: float32 [1024], P('head'), may hold values from -6 to 6
- grouped_layer_scaling: float32 [1024], P('head'), may hold values from 0.5 to 1.5
- attention_exit_projection: bfloat16 [1024, 2048], P('head'), may hold values from -0.1875 to 0.1875
- feedforward_address_proj: bfloat16 [2048, 3584], P(None, 'head'), may hold values from -0.125 to 0.125
- feedforward_content_proj: bfloat16 [3584, 2048], P('head'), may hold values from -0.09375 to 0.09375
Outputs:
- next_tokens: bfloat16 [512, 4, 2048], P('grp', None, 'head')
- next_state: float32 [512, 16, 64, 64], P('grp', 'head')
- next_shift: float32 [512, 2, 2048], P('grp', None, 'head')
Inputs may be any that keep to these rules, and one draw needn't show every extreme that they name: former_indices[g * 8 + j] = ((g + offset_j) mod 64) * 8 + local_j, where the 8 offsets offset_j are distinct numbers of 0 to 63 and local_j is a permutation of 0 to 7, both the same for every group g. `reconstruct_marks`: among the 8 requests of one group at most 2 are marked, and some group has exactly 2.
All inputs are finite; a program needn't handle non-finite values.
Results may differ from a plain program's by a relative error of at most 0.028.
Values may be sent and summed in bfloat16 or wider, within the bound.
No kernel may reach another device: no remote copies, remote signals or barrier semaphores. Data moves between devices by JAX's collectives and lax.ppermute only.
A program may use at most 128 MiB of HBM per device.

v0:
```python
import jax
import jax.numpy as jnp
from jax import lax
from jax.sharding import PartitionSpec as P

ATTENTION_WIDTH = 64
REB = 2
EPSILON = 1e-05


def shifted_2(value, axis, steps):
    count = lax.axis_size(axis)
    pairs = [(source, (source + steps) % count) for source in range(count)]
    return lax.ppermute(value, axis, pairs)


def layer_norm(inputs, gain):
    centered = inputs - jnp.mean(inputs, axis=-1, keepdims=True)
    spread = jnp.mean(centered * centered, axis=-1, keepdims=True)
    return (centered * lax.rsqrt(spread + EPSILON) * gain).astype(jnp.bfloat16)


def blend_rows(current, previous, rate):
    return (current + (previous - current) * rate).astype(jnp.bfloat16)


def project(inputs, weight):
    flat_rows = inputs.reshape(-1, inputs.shape[-1])
    result = jnp.dot(flat_rows, weight, preferred_element_type=jnp.float32)
    return result.reshape(inputs.shape[:-1] + (weight.shape[1],))


def divide_into_groups(inputs):
    return inputs.reshape(inputs.shape[:-1] + (-1, ATTENTION_WIDTH))


def key_value_decay(
    current,
    previous,
    lag_blend_fractions,
    address_projection,
    content_projection,
    fading_lowrank_left,
    fading_lowrank_right,
    fading_baseline_entries,
):
    key_rows = project(blend_rows(current, previous, lag_blend_fractions[1]), address_projection)
    values = project(blend_rows(current, previous, lag_blend_fractions[2]), content_projection)
    lowrank = jnp.tanh(
        project(blend_rows(current, previous, lag_blend_fractions[3]), fading_lowrank_left)
    ).astype(jnp.bfloat16)
    decay_rates = jnp.exp(
        -jnp.exp(fading_baseline_entries + project(lowrank, fading_lowrank_right))
    )
    return (
        divide_into_groups(key_rows),
        divide_into_groups(values),
        divide_into_groups(decay_rates),
    )


def advance(present_outer_product, inputs):
    key_step, value_step, decay_step = inputs
    return (
        decay_step[..., :, None] * present_outer_product
        + key_step[..., :, None] * value_step[..., None, :],
        None,
    )


def rebuild(
    retained_hiddens,
    pre_attention_scaling,
    lag_blend_fractions,
    address_projection,
    content_projection,
    fading_lowrank_left,
    fading_lowrank_right,
    fading_baseline_entries,
):
    standardized_entry = layer_norm(retained_hiddens.astype(jnp.float32), pre_attention_scaling)
    current = standardized_entry.astype(jnp.float32)
    previous = jnp.concatenate([jnp.zeros_like(current[:, :1]), current[:, :-1]], axis=1)
    key_rows, values, decay_rates = key_value_decay(
        current,
        previous,
        lag_blend_fractions,
        address_projection,
        content_projection,
        fading_lowrank_left,
        fading_lowrank_right,
        fading_baseline_entries,
    )
    start_state = jnp.zeros(
        key_rows.shape[:1] + key_rows.shape[2:] + (ATTENTION_WIDTH,), jnp.float32
    )
    final_state, _ = lax.scan(
        advance,
        start_state,
        (jnp.moveaxis(key_rows, 1, 0), jnp.moveaxis(values, 1, 0), jnp.moveaxis(decay_rates, 1, 0)),
    )
    return (final_state, current[:, -1])


def attention_result(
    standardized_entry,
    lagged_entry,
    present_outer_product,
    occupied_slot_totals,
    lag_blend_fractions,
    acceptance_projection,
    address_projection,
    content_projection,
    fading_lowrank_left,
    fading_lowrank_right,
    fading_baseline_entries,
    present_item_reward,
    grouped_layer_scaling,
):
    current = standardized_entry.astype(jnp.float32)
    previous = jnp.concatenate([lagged_entry[:, None], current[:, :-1]], axis=1)
    acceptance_gate_entries = divide_into_groups(
        project(blend_rows(current, previous, lag_blend_fractions[0]), acceptance_projection)
    )
    key_rows, values, decay_rates = key_value_decay(
        current,
        previous,
        lag_blend_fractions,
        address_projection,
        content_projection,
        fading_lowrank_left,
        fading_lowrank_right,
        fading_baseline_entries,
    )
    reward_grouped = divide_into_groups(present_item_reward)
    decoding_results = []
    for query_slot_index in range(current.shape[1]):
        address_content_product = (
            key_rows[:, query_slot_index, :, :, None] * values[:, query_slot_index, :, None, :]
        )
        decoding_results.append(
            jnp.einsum(
                "ghl,ghlm->ghm",
                acceptance_gate_entries[:, query_slot_index],
                present_outer_product + reward_grouped[:, :, None] * address_content_product,
                precision=lax.Precision.HIGHEST,
            )
        )
        valid_rows = (query_slot_index < occupied_slot_totals)[:, None, None, None]
        present_outer_product = jnp.where(
            valid_rows,
            decay_rates[:, query_slot_index, :, :, None] * present_outer_product
            + address_content_product,
            present_outer_product,
        )
    mixed_heads = jnp.stack(decoding_results, axis=1)
    centered = mixed_heads - jnp.mean(mixed_heads, axis=-1, keepdims=True)
    spread = jnp.mean(centered * centered, axis=-1, keepdims=True)
    grouped_results = (
        centered * lax.rsqrt(spread + EPSILON) * divide_into_groups(grouped_layer_scaling)
    ).astype(jnp.bfloat16)
    return (grouped_results.reshape(grouped_results.shape[:2] + (-1,)), present_outer_product)


def last_live(inputs, occupied_slot_totals):
    pick_table = (
        jnp.arange(inputs.shape[1])[None, :, None] == (occupied_slot_totals - 1)[:, None, None]
    )
    return jnp.sum(jnp.where(pick_table, inputs, jnp.zeros_like(inputs)), axis=1)


def on_device(
    arriving_hiddens,
    occupied_slot_totals,
    former_indices,
    reconstruct_marks,
    retained_hiddens,
    carried_memory_matrices,
    lagged_previous_entries,
    pre_attention_scaling,
    pre_feedforward_scaling,
    lag_blend_fractions,
    acceptance_projection,
    address_projection,
    content_projection,
    fading_lowrank_left,
    fading_lowrank_right,
    fading_baseline_entries,
    present_item_reward,
    grouped_layer_scaling,
    attention_exit_projection,
    feedforward_address_proj,
    feedforward_content_proj,
):
    req_rows = arriving_hiddens.shape[0]
    local_heads = carried_memory_matrices.shape[1]
    model_width = pre_attention_scaling.shape[0]
    grp_index = lax.axis_index("grp")
    groups = lax.axis_size("grp")
    head_index = lax.axis_index("head")
    feature_part = model_width // lax.axis_size("head")
    offset = (former_indices // req_rows - grp_index) % groups
    source_row = former_indices % req_rows
    state_size = local_heads * ATTENTION_WIDTH * ATTENTION_WIDTH
    packed = jnp.concatenate(
        [
            carried_memory_matrices.reshape(req_rows, -1),
            lagged_previous_entries.reshape(req_rows, -1),
        ],
        axis=1,
    )
    ready_rows = jnp.take(packed, source_row, axis=0)
    moved_rows = ready_rows
    for bit_index in range((groups - 1).bit_length()):
        shifted = shifted_2(moved_rows, "grp", -(1 << bit_index))
        moved_rows = jnp.where((offset >> bit_index & 1 == 1)[:, None], shifted, moved_rows)
    present_outer_product = moved_rows[:, :state_size].reshape(
        req_rows, local_heads, ATTENTION_WIDTH, ATTENTION_WIDTH
    )
    shift_part = moved_rows[:, state_size:].reshape(req_rows, 2, feature_part)
    mark_rank = jnp.cumsum(reconstruct_marks) - reconstruct_marks
    slot_table = (
        (reconstruct_marks[None, :] == 1) & (mark_rank[None, :] == jnp.arange(REB)[:, None])
    ).astype(jnp.bfloat16)
    chosen = jnp.einsum(
        "sn,ntd->std", slot_table, retained_hiddens, preferred_element_type=jnp.float32
    ).astype(jnp.bfloat16)
    full_tokens, full_chosen = (
        lax.all_gather(arriving_hiddens, "head", axis=2, tiled=True),
        lax.all_gather(chosen, "head", axis=2, tiled=True),
    )
    full_shift = lax.all_gather(shift_part.astype(jnp.bfloat16), "head", axis=2, tiled=True).astype(
        shift_part.dtype
    )
    rebuilt, last_hist = rebuild(
        full_chosen,
        pre_attention_scaling,
        lag_blend_fractions,
        address_projection,
        content_projection,
        fading_lowrank_left,
        fading_lowrank_right,
        fading_baseline_entries,
    )
    pick_slot = jnp.clip(mark_rank, 0, REB - 1)
    marked = reconstruct_marks == 1
    present_outer_product = jnp.where(
        marked[:, None, None, None], jnp.take(rebuilt, pick_slot, axis=0), present_outer_product
    )
    lagged_entry = jnp.where(
        marked[:, None], jnp.take(last_hist, pick_slot, axis=0), full_shift[:, 0]
    )
    standardized_entry = layer_norm(full_tokens.astype(jnp.float32), pre_attention_scaling)
    grouped_results, present_outer_product = attention_result(
        standardized_entry,
        lagged_entry,
        present_outer_product,
        occupied_slot_totals,
        lag_blend_fractions,
        acceptance_projection,
        address_projection,
        content_projection,
        fading_lowrank_left,
        fading_lowrank_right,
        fading_baseline_entries,
        present_item_reward,
        grouped_layer_scaling,
    )
    flat_heads = grouped_results.reshape(-1, grouped_results.shape[-1])
    mix_total = lax.psum(
        jnp.dot(flat_heads, attention_exit_projection, preferred_element_type=jnp.float32).astype(
            jnp.bfloat16
        ),
        "head",
    ).astype(jnp.float32)
    middle = (full_tokens.astype(jnp.float32) + mix_total.reshape(full_tokens.shape)).astype(
        jnp.bfloat16
    )
    middle_local = lax.dynamic_slice_in_dim(middle, head_index * feature_part, feature_part, 2)
    second = layer_norm(middle.astype(jnp.float32), pre_feedforward_scaling)
    current = second.astype(jnp.float32)
    previous = jnp.concatenate([full_shift[:, 1][:, None], current[:, :-1]], axis=1)
    hidden = jnp.square(
        jax.nn.relu(
            project(blend_rows(current, previous, lag_blend_fractions[4]), feedforward_address_proj)
        )
    ).astype(jnp.bfloat16)
    flat_hidden = hidden.reshape(-1, hidden.shape[-1])
    ffn_rows = lax.psum_scatter(
        lax.dot_general(
            feedforward_content_proj,
            flat_hidden,
            (((0,), (1,)), ((), ())),
            preferred_element_type=jnp.float32,
        ).astype(jnp.bfloat16),
        "head",
        scatter_dimension=0,
        tiled=True,
    ).astype(jnp.float32)
    result = (middle_local.astype(jnp.float32) + ffn_rows.T.reshape(middle_local.shape)).astype(
        jnp.bfloat16
    )
    valid_rows = jnp.arange(arriving_hiddens.shape[1])[None, :] < occupied_slot_totals[:, None]
    result = jnp.where(valid_rows[..., None], result, jnp.zeros_like(result))
    time_last = lax.dynamic_slice_in_dim(
        last_live(standardized_entry.astype(jnp.float32), occupied_slot_totals),
        head_index * feature_part,
        feature_part,
        1,
    )
    channel_last = lax.dynamic_slice_in_dim(
        last_live(current, occupied_slot_totals), head_index * feature_part, feature_part, 1
    )
    return (result, present_outer_product, jnp.stack([time_last, channel_last], axis=1))


def solution(mesh):
    placed = (
        P("grp", None, "head"),
        P("grp"),
        P("grp"),
        P("grp"),
        P("grp", None, "head"),
        P("grp", "head", None, None),
        P("grp", None, "head"),
        P(),
        P(),
        P(),
        P(None, "head"),
        P(None, "head"),
        P(None, "head"),
        P(),
        P(None, "head"),
        P("head"),
        P("head"),
        P("head"),
        P("head", None),
        P(None, "head"),
        P("head", None),
    )
    return jax.shard_map(
        on_device,
        mesh=mesh,
        in_specs=placed,
        out_specs=(P("grp", None, "head"), P("grp", "head", None, None), P("grp", None, "head")),
        check_vma=False,
    )
```

profile of v0, /device:TPU:8, one launch (start us, length us, event | category | flops | bytes accessed | tf_op | source)
XLA Modules:
  0.0 305.9 jit_solution(17810951148594460560)
XLA Ops:
  15.0 12.6 %all_gather.10 = bf16[2,32,2048]{2,1,0:T(8,128)(2,1)S(1)} all-gather(bf16[2,32,512]{2,1,0:T(8,128)(2,1)S(1)} %copy.145), channel_id=1, replica_groups=mesh['grp'=64,'head'=4] {'head'}, dimensions={2}, use_global_device_ids=true | all-gather | bytes 327680 | tf_op jit(solution)/shard_map/all_gather | solution.py:230
  30.2 8.3 %collective-permute-start.1 = (f32[8,17408]{1,0:T(8,128)S(1)}, f32[8,17408]{1,0:T(8,128)}, u32[]{:S(2)}, u32[]{:S(2)}) collective-permute-start(f32[8,17408]{1,0:T(8,128)S(1)} %broadcast_select_fusion.1), channel_id=1, source_target_pairs={{0,248},{4,252},{8,0},{12,4},{16,8},{20,12},{24,16},{28,20},{32,24... | collective-permute-start | bytes 1671176 | tf_op jit(solution)/shard_map/ppermute | solution.py:14
  40.1 2.3 copy.80
  43.9 2.4 convolution_bitcast_fusion.1
  46.3 2.4 convolution_bitcast_fusion
  50.0 5.3 %collective-permute-start.2 = (f32[8,17408]{1,0:T(8,128)S(1)}, f32[8,17408]{1,0:T(8,128)}, u32[]{:S(2)}, u32[]{:S(2)}) collective-permute-start(f32[8,17408]{1,0:T(8,128)S(1)} %broadcast_select_fusion.2), channel_id=1, source_target_pairs={{0,240},{4,244},{8,248},{12,252},{16,0},{20,4},{24,8},{28,12},{32,... | collective-permute-start | bytes 1671176 | tf_op jit(solution)/shard_map/ppermute | solution.py:14
  55.4 34.7 %while.11 = (s32[]{:T(128)}, f32[2,4,64,64]{3,2,1,0:T(8,128)S(1)}, f32[32,2,4,64]{3,2,1,0:T(4,128)S(1)}, f32[32,2,4,64]{3,0,2,1:T(8,128)S(1)}, f32[32,2,4,64]{3,0,2,1:T(8,128)}, /*index=5*/s32[]{:T(128)}, s32[]{:T(128)}) while((s32[]{:T(128)}, f32[2,4,64,64]{3,2,1,0:T(8,128)S(1)}, f32[32,2,4,64]{3,2,1,0:T(4,128)S(1)}, ...), condition=%wide.region_6.7_spmd.clone, body=%wide.region_5.6_spmd.clone.sunk | while | flops 131075 | bytes 280679 | solution.py:97
  92.4 2.3 copy.77
  94.7 12.0 %all_gather.9 = bf16[8,4,2048]{2,1,0:T(4,128)(2,1)S(1)} all-gather(bf16[8,4,512]{2,1,0:T(4,128)(2,1)S(1)} %copy-done.16), channel_id=1, replica_groups=mesh['grp'=64,'head'=4] {'head'}, dimensions={2}, use_global_device_ids=true | all-gather | bytes 163840 | tf_op jit(solution)/shard_map/all_gather | solution.py:229
  108.7 18.3 %collective-permute-done.3 = f32[8,17408]{1,0:T(8,128)S(1)} collective-permute-done((f32[8,17408]{1,0:T(8,128)S(1)}, f32[8,17408]{1,0:T(8,128)S(1)}, u32[]{:S(2)}, u32[]{:S(2)}) %collective-permute-start.3) | collective-permute-done | bytes 557088 | tf_op jit(solution)/shard_map/ppermute | solution.py:14
  128.1 38.4 %collective-permute-done.4 = f32[8,17408]{1,0:T(8,128)S(1)} collective-permute-done((f32[8,17408]{1,0:T(8,128)S(1)}, f32[8,17408]{1,0:T(8,128)S(1)}, u32[]{:S(2)}, u32[]{:S(2)}) %collective-permute-start.4) | collective-permute-done | bytes 557088 | tf_op jit(solution)/shard_map/ppermute | solution.py:14
  168.1 18.2 %collective-permute-done.5 = f32[8,17408]{1,0:T(8,128)} collective-permute-done((f32[8,17408]{1,0:T(8,128)S(1)}, f32[8,17408]{1,0:T(8,128)}, u32[]{:S(2)}, u32[]{:S(2)}) %collective-permute-start.5) | collective-permute-done | bytes 557088 | tf_op jit(solution)/shard_map/ppermute | solution.py:14
  188.4 12.0 %all_gather.11 = bf16[8,2,2048]{2,0,1:T(8,128)(2,1)S(1)} all-gather(bf16[8,2,512]{2,0,1:T(8,128)(2,1)S(1)} %bitcast.193), channel_id=1, replica_groups=mesh['grp'=64,'head'=4] {'head'}, dimensions={2}, use_global_device_ids=true | all-gather | bytes 81920 | tf_op jit(solution)/shard_map/all_gather | solution.py:232
  205.2 1.9 fusion.105
  207.1 1.9 fusion.103
  209.1 1.8 fusion.101
  211.0 4.1 %fusion.36 = (f32[8,4,64,64]{3,2,1,0:T(8,128)}, f32[8,4,64,64]{3,2,1,0:T(8,128)S(1)}) fusion(f32[8,4,64]{2,1,0:T(4,128)S(1)} %copy-done.13, f32[8,4,64]{2,1,0:T(4,128)S(1)} %copy.94, f32[8,4,64]{2,1,0:T(4,128)S(1)} %copy.93, f32[8,4,64]{2,1,0:T(4,128)S(1)} %copy-done.12, f32[8,4,64]{2,1,0:T(4,128)S(1)} %copy.92, f32[8,4,64]{2,1,0:T(4,128)S(1)} %copy.91, ...), kind=kLoop, calls=%fused_computation.49 | loop fusion | flops 2359296 | bytes 2195504 | tf_op jit(solution)/shard_map/jit(_where)/select_n | solution.py:150
  215.2 2.8 fusion.34
  218.0 2.3 fusion.30
  220.3 1.7 fusion.26
  225.3 40.4 %all-reduce.3.cloned.1.call-done = bf16[8,4,2048]{2,1,0:T(4,128)(2,1)} async-done(((bf16[8,4,2048]{2,1,0:T(4,128)(2,1)}), bf16[8,4,2048]{2,1,0:T(4,128)(2,1)}) %all-reduce.3.cloned.1.call-update) | async-done | bytes 131088 | tf_op jit(solution)/shard_map/psum | solution.py:270
  267.8 2.7 fusion.10
  270.6 3.4 %fusion.3 = bf16[2048,32]{0,1:T(8,128)(2,1)} fusion(bf16[32,896]{1,0:T(8,128)(2,1)S(1)} %reshape.296, bf16[896,2048]{1,0:T(8,128)(2,1)} %param.43), kind=kOutput, calls=%fused_computation.12 | convolution fusion | flops 117506048 | bytes 3858432 | tf_op jit(solution)/shard_map/dot_general | solution.py:290
  274.7 22.9 %reduce-scatter.2.cloned.1.call-done = bf16[512,32]{0,1:T(8,128)(2,1)} async-done(((bf16[2048,32]{0,1:T(8,128)(2,1)}), bf16[512,32]{0,1:T(8,128)(2,1)}) %reduce-scatter.2.cloned.1.call-update) | async-done | bytes 32784 | tf_op jit(solution)/shard_map/reduce_scatter | solution.py:289
  (274 shorter events, 69.7 us)
Async XLA Ops:
  7.2 216.6 %copy-start = (bf16[256,2048]{1,0:T(8,128)(2,1)S(1)}, bf16[256,2048]{1,0:T(8,128)(2,1)}, u32[]{:S(2)}) copy-start(bf16[256,2048]{1,0:T(8,128)(2,1)} %param.41) | copy-start | bytes 3145732
  7.2 258.5 %all-reduce.3.cloned.1.call-start = ((), (), s32[]{:S(2)}) async-start(), calls=%async_computation.1 | async-start | bytes 262144 | tf_op jit(solution)/shard_map/psum | solution.py:270
  11.8 26.7 %copy-start.17 = (bf16[64,256]{1,0:T(8,128)(2,1)S(1)}, bf16[64,256]{1,0:T(8,128)(2,1)}, u32[]{:S(2)}) copy-start(bf16[64,256]{1,0:T(8,128)(2,1)} %param.37) | copy-start | bytes 98308
  11.8 26.7 %copy-start.30 = (f32[256]{0:T(256)S(1)}, f32[256]{0:T(256)}, u32[]{:S(2)}) copy-start(f32[256]{0:T(256)} %param.38) | copy-start | bytes 3076
  12.7 15.4 %collective-permute-start = (f32[8,17408]{1,0:T(8,128)}, f32[8,17408]{1,0:T(8,128)S(1)}, u32[]{:S(2)}, u32[]{:S(2)}) collective-permute-start(f32[8,17408]{1,0:T(8,128)} %broadcast_select_fusion), channel_id=1, source_target_pairs={{0,252},{4,0},{8,4},{12,8},{16,12},{20,16},{24,20},{28,24},{32,28}... | collective-permute-start | bytes 1671176 | tf_op jit(solution)/shard_map/ppermute | solution.py:14
  13.5 187.6 %copy-start.19 = (pred[8]{0:T(512)(128)(4,1)}, pred[8]{0:T(512)(128)(4,1)S(1)}, u32[]{:S(2)}) copy-start(pred[8]{0:T(512)(128)(4,1)S(1)} %get-tuple-element.124) | copy-start | bytes 28
  30.2 18.5 %collective-permute-start.1 = (f32[8,17408]{1,0:T(8,128)S(1)}, f32[8,17408]{1,0:T(8,128)}, u32[]{:S(2)}, u32[]{:S(2)}) collective-permute-start(f32[8,17408]{1,0:T(8,128)S(1)} %broadcast_select_fusion.1), channel_id=1, source_target_pairs={{0,248},{4,252},{8,0},{12,4},{16,8},{20,12},{24,16},{28,20},{32,24... | collective-permute-start | bytes 1671176 | tf_op jit(solution)/shard_map/ppermute | solution.py:14
  48.7 46.0 %copy-start.16 = (bf16[8,4,512]{2,1,0:T(4,128)(2,1)S(1)}, bf16[8,4,512]{2,1,0:T(4,128)(2,1)}, u32[]{:S(2)}) copy-start(bf16[8,4,512]{2,1,0:T(4,128)(2,1)} %param.23) | copy-start | bytes 98308
  50.0 58.1 %copy-start.35 = (s32[8]{0:T(128)S(1)}, s32[8]{0:T(128)}, u32[]{:S(2)}) copy-start(s32[8]{0:T(128)} %param.24) | copy-start | bytes 100
  50.0 56.6 %collective-permute-start.2 = (f32[8,17408]{1,0:T(8,128)S(1)}, f32[8,17408]{1,0:T(8,128)}, u32[]{:S(2)}, u32[]{:S(2)}) collective-permute-start(f32[8,17408]{1,0:T(8,128)S(1)} %broadcast_select_fusion.2), channel_id=1, source_target_pairs={{0,240},{4,244},{8,248},{12,252},{16,0},{20,4},{24,8},{28,12},{32,... | collective-permute-start | bytes 1671176 | tf_op jit(solution)/shard_map/ppermute | solution.py:14
  90.1 76.4 %copy-start.24 = (pred[8]{0:T(512)(128)(4,1)S(1)}, pred[8]{0:T(512)(128)(4,1)}, u32[]{:S(2)}) copy-start(pred[8]{0:T(512)(128)(4,1)} %get-tuple-element.125) | copy-start | bytes 28
  92.4 74.3 %copy-start.29 = (s32[8]{0:T(128)S(1)}, s32[8]{0:T(128)}, u32[]{:S(2)}) copy-start(s32[8]{0:T(128)} %get-tuple-element.87) | copy-start | bytes 100
  107.9 78.5 %copy-start.28 = (pred[8]{0:T(512)(128)(4,1)S(1)}, pred[8]{0:T(512)(128)(4,1)}, u32[]{:S(2)}) copy-start(pred[8]{0:T(512)(128)(4,1)} %get-tuple-element.89) | copy-start | bytes 28
  107.9 19.1 %collective-permute-start.3 = (f32[8,17408]{1,0:T(8,128)S(1)}, f32[8,17408]{1,0:T(8,128)S(1)}, u32[]{:S(2)}, u32[]{:S(2)}) collective-permute-start(f32[8,17408]{1,0:T(8,128)S(1)} %broadcast_select_fusion.3), channel_id=1, source_target_pairs={{0,224},{4,228},{8,232},{12,236},{16,240},{20,244},{24,248},{28,25... | collective-permute-start | bytes 1671176 | tf_op jit(solution)/shard_map/ppermute | solution.py:14
  127.1 39.4 %collective-permute-start.4 = (f32[8,17408]{1,0:T(8,128)S(1)}, f32[8,17408]{1,0:T(8,128)S(1)}, u32[]{:S(2)}, u32[]{:S(2)}) collective-permute-start(f32[8,17408]{1,0:T(8,128)S(1)} %broadcast_select_fusion.4), channel_id=1, source_target_pairs={{0,192},{4,196},{8,200},{12,204},{16,208},{20,212},{24,216},{28,22... | collective-permute-start | bytes 1671176 | tf_op jit(solution)/shard_map/ppermute | solution.py:14
  166.5 34.6 %copy-start.23 = (pred[8]{0:T(512)(128)(4,1)S(1)}, pred[8]{0:T(512)(128)(4,1)}, u32[]{:S(2)}) copy-start(pred[8]{0:T(512)(128)(4,1)} %get-tuple-element.86) | copy-start | bytes 28
  166.5 34.7 %copy-start.22 = (f32[1,2048]{1,0:T(1,128)S(1)}, f32[1,2048]{1,0:T(1,128)}, u32[]{:S(2)}) copy-start(f32[1,2048]{1,0:T(1,128)} %copy-done.21) | copy-start | bytes 24580
  166.5 34.7 %copy-start.36 = (bf16[2048,64]{0,1:T(8,128)(2,1)S(1)}, bf16[2048,64]{0,1:T(8,128)(2,1)}, u32[]{:S(2)}) copy-start(bf16[2048,64]{0,1:T(8,128)(2,1)} %param.36) | copy-start | bytes 786436
  166.6 19.7 %collective-permute-start.5 = (f32[8,17408]{1,0:T(8,128)S(1)}, f32[8,17408]{1,0:T(8,128)}, u32[]{:S(2)}, u32[]{:S(2)}) collective-permute-start(f32[8,17408]{1,0:T(8,128)S(1)} %broadcast_select_fusion.5), channel_id=1, source_target_pairs={{0,128},{4,132},{8,136},{12,140},{16,144},{20,148},{24,152},{28,15... | collective-permute-start | bytes 1671176 | tf_op jit(solution)/shard_map/ppermute | solution.py:14
  167.3 34.4 %copy-start.31 = (f32[256]{0:T(256)S(1)}, f32[256]{0:T(256)}, u32[]{:S(2)}) copy-start(f32[256]{0:T(256)} %param.38) | copy-start | bytes 3076
  220.3 46.7 %copy-start.14 = (f32[2048]{0:T(1024)S(1)}, f32[2048]{0:T(1024)}, u32[]{:S(2)}) copy-start(f32[2048]{0:T(1024)} %param.31) | copy-start | bytes 24580
  220.3 46.9 %copy-start.15 = (f32[1,2048]{1,0:T(1,128)S(1)}, f32[1,2048]{1,0:T(1,128)}, u32[]{:S(2)}) copy-start(f32[1,2048]{1,0:T(1,128)} %get-tuple-element.99) | copy-start | bytes 24580
  224.8 72.8 %reduce-scatter.2.cloned.1.call-start = ((), (), s32[]{:S(2)}) async-start(), calls=%async_computation.2 | async-start | bytes 163840 | tf_op jit(solution)/shard_map/reduce_scatter | solution.py:289
  270.5 27.9 %copy-start.32 = (pred[8,4]{1,0:T(8,128)(4,1)S(1)}, pred[8,4]{1,0:T(8,128)(4,1)}, u32[]{:S(2)}) copy-start(pred[8,4]{1,0:T(8,128)(4,1)} %iota_compare_fusion.1) | copy-start | bytes 100
  (22 other events, 168.7 us)
Sparse Core Ops, SparseCore 0:
  225.0 40.6 all-reduce.2
  274.2 23.3 reduce-scatter.1
where the time goes:
time: 309 us; the launch traced here: 306 us
  waiting for transfers between devices  138 us (45%)
  local copies, waits for them, and re-layouts  44.9 us (15%)
  blocking collectives  36.6 us (12%)
  other arithmetic  29.1 us (9%)
  matrix products  27 us (9%)
  between operations  14.9 us (5%)
  starting transfers between devices  14.1 us (5%)
    ppermute x6, waiting for transfers between devices, shifted_2(): return lax.ppermute(value, axis, pairs)  74.9 us
    psum x1, waiting for transfers between devices, on_device(): lax.psum(jnp.dot(flat_heads, attention_exit_projection, preferred_element...  40.4 us
    dynamic_slice x32, local copies, waits for them, and re-layouts, rebuild(): lax.scan(advance, start_state, (jnp.moveaxis(key_rows, 1, 0), jnp.moveaxi...  24.8 us
    reduce_scatter x1, waiting for transfers between devices, on_device(): lax.psum_scatter(lax.dot_general(feedforward_content_proj, flat_hidden, (...  22.9 us
    dot_general x9, matrix products, project(): result = jnp.dot(flat_rows, weight, preferred_element_type=jnp.float32)  15.1 us
    ppermute x6, starting transfers between devices, shifted_2(): return lax.ppermute(value, axis, pairs)  13.8 us
    all_gather x1, blocking collectives, on_device(): lax.all_gather(chosen, 'head', axis=2, tiled=True)  12.6 us
    all_gather x1, blocking collectives, on_device(): lax.all_gather(shift_part.astype(jnp.bfloat16), 'head', axis=2, tiled=True)  12 us
  transfers between devices with their start and end apart: 8, of which 5 were waited for; matrix products, arithmetic and copies ran while one was open for 18% of the time, Pallas kernels for 0%

commit v1 on v0

--- a/solution.py
+++ b/solution.py
@@ -6,6 +6,19 @@
 ATTENTION_WIDTH = 64
 REB = 2
 EPSILON = 1e-05
+
+
+def ring_gather(x, axis, dim):
+    ways = lax.axis_size(axis)
+    up = [(d, (d + 1) % ways) for d in range(ways)]
+    down = [(d, (d - 1) % ways) for d in range(ways)]
+    earlier, later = ([x], [x])
+    for _ in range(ways // 2):
+        earlier.append(lax.ppermute(earlier[-1], axis, up))
+    for _ in range((ways - 1) // 2):
+        later.append(lax.ppermute(later[-1], axis, down))
+    line = jnp.concatenate([*earlier[::-1], *later[1:]], axis=dim)
+    return jnp.roll(line, (lax.axis_index(axis) - ways // 2) * x.shape[dim], axis=dim)
 
 
 def shifted_2(value, axis, steps):
@@ -227,7 +240,7 @@
     ).astype(jnp.bfloat16)
     full_tokens, full_chosen = (
         lax.all_gather(arriving_hiddens, "head", axis=2, tiled=True),
-        lax.all_gather(chosen, "head", axis=2, tiled=True),
+        ring_gather(chosen, "head", 2),
     )
     full_shift = lax.all_gather(shift_part.astype(jnp.bfloat16), "head", axis=2, tiled=True).astype(
         shift_part.dtype

time: 309 us -> 333 us (1.078)
  local copies, waits for them, and re-layouts: 44.9 us -> 65 us
  blocking collectives: 36.6 us -> 28.8 us
  waiting for transfers between devices: 138 us -> 145 us
    mul x32, local copies, waits for them, and re-layouts: 0.23 us -> 21.9 us  [advance(): decay_step[..., :, None] * present_outer_product]
    all_gather x1 -> x0, blocking collectives: 12.6 us -> none  [on_device(): lax.all_gather(chosen, 'head', axis=2, tiled=True)]
    psum x1, waiting for transfers between devices: 40.4 us -> 50.1 us  [on_device(): lax.psum(jnp.dot(flat_heads, attention_exit_projection, preferred_element...]
    ppermute x6, waiting for transfers between devices: 74.9 us -> 68.8 us  [shifted_2(): return lax.ppermute(value, axis, pairs)]
    ppermute x6, starting transfers between devices: 13.8 us -> 8.33 us  [shifted_2(): return lax.ppermute(value, axis, pairs)]
    ppermute x0 -> x3, starting transfers between devices: none -> 4.85 us  [the longest x1 2.76 us: ring_gather(): later.append(lax.ppermute(later[-1], axis, down))]
    all_gather x1, blocking collectives: 12 us -> 16.8 us  [on_device(): lax.all_gather(shift_part.astype(jnp.bfloat16), 'head', axis=2, tiled=True)]
    unnamed x82 -> x81, local copies, waits for them, and re-layouts: 9.13 us -> 6.83 us
  transfers between devices with their start and end apart: 8 -> 11, of which waited for: 5 -> 7; matrix products, arithmetic and copies ran while one was open for 18% -> 25% of each run, Pallas kernels for 0% -> 0%
where the time goes in v1:
time: 333 us; the launch traced here: 329 us
  waiting for transfers between devices  145 us (44%)
  local copies, waits for them, and re-layouts  65 us (20%)
  other arithmetic  31.4 us (9%)
  matrix products  29.6 us (9%)
  blocking collectives  28.8 us (9%)
  between operations  14.9 us (4%)
  starting transfers between devices  13.5 us (4%)
    ppermute x6, waiting for transfers between devices, shifted_2(): return lax.ppermute(value, axis, pairs)  68.8 us
    psum x1, waiting for transfers between devices, on_device(): lax.psum(jnp.dot(flat_heads, attention_exit_projection, preferred_element...  50.1 us
    dynamic_slice x32, local copies, waits for them, and re-layouts, rebuild(): lax.scan(advance, start_state, (jnp.moveaxis(key_rows, 1, 0), jnp.moveaxi...  25 us
    reduce_scatter x1, waiting for transfers between devices, on_device(): lax.psum_scatter(lax.dot_general(feedforward_content_proj, flat_hidden, (...  22.9 us
    mul x32, local copies, waits for them, and re-layouts, advance(): decay_step[..., :, None] * present_outer_product  21.9 us
    all_gather x1, blocking collectives, on_device(): lax.all_gather(shift_part.astype(jnp.bfloat16), 'head', axis=2, tiled=True)  16.8 us
    dot_general x9, matrix products, project(): result = jnp.dot(flat_rows, weight, preferred_element_type=jnp.float32)  16.7 us
    all_gather x1, blocking collectives, on_device(): lax.all_gather(arriving_hiddens, 'head', axis=2, tiled=True)  12 us
  transfers between devices with their start and end apart: 11, of which 7 were waited for; matrix products, arithmetic and copies ran while one was open for 25% of the time, Pallas kernels for 0%

profile of v1, /device:TPU:8, one launch (start us, length us, event | category | flops | bytes accessed | tf_op | source)
XLA Modules:
  0.0 328.6 jit_solution(14530247216234283973)
XLA Ops:
  11.2 2.8 collective-permute-start.2
  21.3 12.0 %all_gather.6 = bf16[8,4,2048]{2,1,0:T(4,128)(2,1)S(1)} all-gather(bf16[8,4,512]{2,1,0:T(4,128)(2,1)S(1)} %copy-done.11), channel_id=1, replica_groups=mesh['grp'=64,'head'=4] {'head'}, dimensions={2}, use_global_device_ids=true | all-gather | bytes 163840 | tf_op jit(solution)/shard_map/all_gather | solution.py:242
  35.1 2.3 copy.77
  40.3 2.1 collective-permute-start.1
  43.1 2.8 collective-permute-done.1
  47.1 8.0 %collective-permute-start.4 = (f32[8,17408]{1,0:T(8,128)S(1)}, f32[8,17408]{1,0:T(8,128)S(1)}, u32[]{:S(2)}, u32[]{:S(2)}) collective-permute-start(f32[8,17408]{1,0:T(8,128)S(1)} %broadcast_select_fusion.1), channel_id=1, source_target_pairs={{0,248},{4,252},{8,0},{12,4},{16,8},{20,12},{24,16},{28,20},{32,24... | collective-permute-start | bytes 1671176 | tf_op jit(solution)/shard_map/ppermute | solution.py:27
  55.1 18.9 %collective-permute-done.4 = f32[8,17408]{1,0:T(8,128)S(1)} collective-permute-done((f32[8,17408]{1,0:T(8,128)S(1)}, f32[8,17408]{1,0:T(8,128)S(1)}, u32[]{:S(2)}, u32[]{:S(2)}) %collective-permute-start.4) | collective-permute-done | bytes 557088 | tf_op jit(solution)/shard_map/ppermute | solution.py:27
  74.7 10.8 %collective-permute-done.5 = f32[8,17408]{1,0:T(8,128)S(1)} collective-permute-done((f32[8,17408]{1,0:T(8,128)S(1)}, f32[8,17408]{1,0:T(8,128)S(1)}, u32[]{:S(2)}, u32[]{:S(2)}) %collective-permute-start.5) | collective-permute-done | bytes 557088 | tf_op jit(solution)/shard_map/ppermute | solution.py:27
  87.3 18.5 %collective-permute-done.6 = f32[8,17408]{1,0:T(8,128)S(1)} collective-permute-done((f32[8,17408]{1,0:T(8,128)S(1)}, f32[8,17408]{1,0:T(8,128)S(1)}, u32[]{:S(2)}, u32[]{:S(2)}) %collective-permute-start.6) | collective-permute-done | bytes 557088 | tf_op jit(solution)/shard_map/ppermute | solution.py:27
  108.6 2.8 convolution_bitcast_fusion.1
  111.4 2.4 convolution_bitcast_fusion
  113.8 20.6 %collective-permute-done.7 = f32[8,17408]{1,0:T(8,128)} collective-permute-done((f32[8,17408]{1,0:T(8,128)S(1)}, f32[8,17408]{1,0:T(8,128)}, u32[]{:S(2)}, u32[]{:S(2)}) %collective-permute-start.7) | collective-permute-done | bytes 557088 | tf_op jit(solution)/shard_map/ppermute | solution.py:27
  135.7 56.4 %while.11 = (s32[]{:T(128)}, f32[2,4,64,64]{3,2,1,0:T(8,128)S(1)}, f32[32,2,4,64]{3,2,1,0:T(4,128)}, f32[32,2,4,64]{3,0,2,1:T(8,128)}, f32[32,2,4,64]{3,0,2,1:T(8,128)}, /*index=5*/s32[]{:T(128)}, s32[]{:T(128)}) while((s32[]{:T(128)}, f32[2,4,64,64]{3,2,1,0:T(8,128)S(1)}, f32[32,2,4,64]{3,2,1,0:T(4,128)}, ...), condition=%wide.region_6.7_spmd.clone, body=%wide.region_5.6_spmd.clone.sunk | while | flops 131075 | bytes 280679 | solution.py:110
  196.3 16.8 %all_gather.7 = bf16[8,2,2048]{2,0,1:T(8,128)(2,1)S(1)} all-gather(bf16[8,2,512]{2,0,1:T(8,128)(2,1)S(1)} %bitcast.193), channel_id=1, replica_groups=mesh['grp'=64,'head'=4] {'head'}, dimensions={2}, use_global_device_ids=true | all-gather | bytes 81920 | tf_op jit(solution)/shard_map/all_gather | solution.py:245
  218.2 1.9 fusion.105
  220.1 1.9 fusion.103
  222.1 1.8 fusion.101
  224.0 4.1 %fusion.36 = (f32[8,4,64,64]{3,2,1,0:T(8,128)}, f32[8,4,64,64]{3,2,1,0:T(8,128)S(1)}) fusion(f32[8,4,64]{2,1,0:T(4,128)S(1)} %copy-done.8, f32[8,4,64]{2,1,0:T(4,128)S(1)} %copy.94, f32[8,4,64]{2,1,0:T(4,128)S(1)} %copy.93, f32[8,4,64]{2,1,0:T(4,128)S(1)} %copy-done.7, f32[8,4,64]{2,1,0:T(4,128)S(1)} %copy.92, f32[8,4,64]{2,1,0:T(4,128)S(1)} %copy.91, ...), kind=kLoop, calls=%fused_computation.49 | loop fusion | flops 2359296 | bytes 2195504 | tf_op jit(solution)/shard_map/jit(_where)/select_n | solution.py:163
  228.1 2.8 fusion.34
  231.0 2.3 fusion.30
  238.2 50.1 %all-reduce.3.cloned.1.call-done = bf16[8,4,2048]{2,1,0:T(4,128)(2,1)} async-done(((bf16[8,4,2048]{2,1,0:T(4,128)(2,1)}), bf16[8,4,2048]{2,1,0:T(4,128)(2,1)}) %all-reduce.3.cloned.1.call-update) | async-done | bytes 131088 | tf_op jit(solution)/shard_map/psum | solution.py:283
  290.5 2.7 fusion.10
  293.3 3.4 %fusion.3 = bf16[2048,32]{0,1:T(8,128)(2,1)} fusion(bf16[32,896]{1,0:T(8,128)(2,1)S(1)} %reshape.296, bf16[896,2048]{1,0:T(8,128)(2,1)} %param.43), kind=kOutput, calls=%fused_computation.12 | convolution fusion | flops 117506048 | bytes 3858432 | tf_op jit(solution)/shard_map/dot_general | solution.py:303
  297.4 22.9 %reduce-scatter.2.cloned.1.call-done = bf16[512,32]{0,1:T(8,128)(2,1)} async-done(((bf16[2048,32]{0,1:T(8,128)(2,1)}), bf16[512,32]{0,1:T(8,128)(2,1)}) %reduce-scatter.2.cloned.1.call-update) | async-done | bytes 32784 | tf_op jit(solution)/shard_map/reduce_scatter | solution.py:302
  (279 shorter events, 98.3 us)
Async XLA Ops:
  7.2 229.6 %copy-start = (bf16[256,2048]{1,0:T(8,128)(2,1)S(1)}, bf16[256,2048]{1,0:T(8,128)(2,1)}, u32[]{:S(2)}) copy-start(bf16[256,2048]{1,0:T(8,128)(2,1)} %param.41) | copy-start | bytes 3145732
  7.2 281.2 %all-reduce.3.cloned.1.call-start = ((), (), s32[]{:S(2)}) async-start(), calls=%async_computation.1 | async-start | bytes 262144 | tf_op jit(solution)/shard_map/psum | solution.py:283
  11.2 43.9 %collective-permute-start.2 = (bf16[2,32,512]{2,1,0:T(8,128)(2,1)}, bf16[2,32,512]{2,1,0:T(8,128)(2,1)S(1)}, u32[]{:S(2)}, u32[]{:S(2)}) collective-permute-start(bf16[2,32,512]{2,1,0:T(8,128)(2,1)} %copy.145), channel_id=1, source_target_pairs={{0,3},{1,0},{2,1},{3,2},{4,7},{5,4},{6,5},{7,6},{8,11},{9,8},{10,9... | collective-permute-start | bytes 196616 | tf_op jit(solution)/shard_map/ppermute | solution.py:19
  14.0 26.3 %collective-permute-start = (bf16[2,32,512]{2,1,0:T(8,128)(2,1)}, bf16[2,32,512]{2,1,0:T(8,128)(2,1)S(1)}, u32[]{:S(2)}, u32[]{:S(2)}) collective-permute-start(bf16[2,32,512]{2,1,0:T(8,128)(2,1)} %copy.145), channel_id=1, source_target_pairs={{0,1},{1,2},{2,3},{3,0},{4,5},{5,6},{6,7},{7,4},{8,9},{9,10},{10,1... | collective-permute-start | bytes 196616 | tf_op jit(solution)/shard_map/ppermute | solution.py:17
  19.4 26.5 %collective-permute-start.3 = (f32[8,17408]{1,0:T(8,128)}, f32[8,17408]{1,0:T(8,128)}, u32[]{:S(2)}, u32[]{:S(2)}) collective-permute-start(f32[8,17408]{1,0:T(8,128)} %broadcast_select_fusion), channel_id=1, source_target_pairs={{0,252},{4,0},{8,4},{12,8},{16,12},{20,16},{24,20},{28,24},{32,28}... | collective-permute-start | bytes 1671176 | tf_op jit(solution)/shard_map/ppermute | solution.py:27
  37.4 36.7 %copy-start.22 = (pred[8]{0:T(512)(128)(4,1)S(1)}, pred[8]{0:T(512)(128)(4,1)}, u32[]{:S(2)}) copy-start(pred[8]{0:T(512)(128)(4,1)} %get-tuple-element.126) | copy-start | bytes 28
  40.3 71.1 %copy-start.1 = (bf16[2048,256]{0,1:T(8,128)(2,1)}, bf16[2048,256]{0,1:T(8,128)(2,1)S(1)}, u32[]{:S(2)}) copy-start(bf16[2048,256]{0,1:T(8,128)(2,1)S(1)} %copy.81) | copy-start | bytes 3145732
  40.3 5.6 %collective-permute-start.1 = (bf16[2,32,512]{2,1,0:T(8,128)(2,1)S(1)}, bf16[2,32,512]{2,1,0:T(8,128)(2,1)S(1)}, u32[]{:S(2)}, u32[]{:S(2)}) collective-permute-start(bf16[2,32,512]{2,1,0:T(8,128)(2,1)S(1)} %collective-permute-done), channel_id=1, source_target_pairs={{0,1},{1,2},{2,3},{3,0},{4,5},{5,6},{6,7},{7,4},{8,9},{9,10},{10,1... | collective-permute-start | bytes 196616 | tf_op jit(solution)/shard_map/ppermute | solution.py:17
  43.1 62.7 %copy-start.21 = (pred[8]{0:T(512)(128)(4,1)S(1)}, pred[8]{0:T(512)(128)(4,1)}, u32[]{:S(2)}) copy-start(pred[8]{0:T(512)(128)(4,1)} %get-tuple-element.128) | copy-start | bytes 28
  47.1 27.0 %collective-permute-start.4 = (f32[8,17408]{1,0:T(8,128)S(1)}, f32[8,17408]{1,0:T(8,128)S(1)}, u32[]{:S(2)}, u32[]{:S(2)}) collective-permute-start(f32[8,17408]{1,0:T(8,128)S(1)} %broadcast_select_fusion.1), channel_id=1, source_target_pairs={{0,248},{4,252},{8,0},{12,4},{16,8},{20,12},{24,16},{28,20},{32,24... | collective-permute-start | bytes 1671176 | tf_op jit(solution)/shard_map/ppermute | solution.py:27
  74.2 11.3 %collective-permute-start.5 = (f32[8,17408]{1,0:T(8,128)S(1)}, f32[8,17408]{1,0:T(8,128)S(1)}, u32[]{:S(2)}, u32[]{:S(2)}) collective-permute-start(f32[8,17408]{1,0:T(8,128)S(1)} %broadcast_select_fusion.2), channel_id=1, source_target_pairs={{0,240},{4,244},{8,248},{12,252},{16,0},{20,4},{24,8},{28,12},{32,... | collective-permute-start | bytes 1671176 | tf_op jit(solution)/shard_map/ppermute | solution.py:27
  74.3 31.6 %copy-start.2 = (bf16[2,32,4096]{2,1,0:T(8,128)(2,1)}, bf16[2,32,4096]{2,1,0:T(8,128)(2,1)S(1)}, u32[]{:S(2)}) copy-start(bf16[2,32,4096]{2,1,0:T(8,128)(2,1)S(1)} %constant_dynamic-update-slice_fusion) | copy-start | bytes 1572868
  86.3 19.6 %collective-permute-start.6 = (f32[8,17408]{1,0:T(8,128)S(1)}, f32[8,17408]{1,0:T(8,128)S(1)}, u32[]{:S(2)}, u32[]{:S(2)}) collective-permute-start(f32[8,17408]{1,0:T(8,128)S(1)} %broadcast_select_fusion.3), channel_id=1, source_target_pairs={{0,224},{4,228},{8,232},{12,236},{16,240},{20,244},{24,248},{28,25... | collective-permute-start | bytes 1671176 | tf_op jit(solution)/shard_map/ppermute | solution.py:27
  106.0 28.4 %collective-permute-start.7 = (f32[8,17408]{1,0:T(8,128)S(1)}, f32[8,17408]{1,0:T(8,128)}, u32[]{:S(2)}, u32[]{:S(2)}) collective-permute-start(f32[8,17408]{1,0:T(8,128)S(1)} %broadcast_select_fusion.4), channel_id=1, source_target_pairs={{0,192},{4,196},{8,200},{12,204},{16,208},{20,212},{24,216},{28,22... | collective-permute-start | bytes 1671176 | tf_op jit(solution)/shard_map/ppermute | solution.py:27
  134.4 59.9 %copy-start.26 = (pred[8]{0:T(512)(128)(4,1)S(1)}, pred[8]{0:T(512)(128)(4,1)}, u32[]{:S(2)}) copy-start(pred[8]{0:T(512)(128)(4,1)} %get-tuple-element.89) | copy-start | bytes 28
  135.6 58.7 %collective-permute-start.8 = (f32[8,17408]{1,0:T(8,128)S(1)}, f32[8,17408]{1,0:T(8,128)}, u32[]{:S(2)}, u32[]{:S(2)}) collective-permute-start(f32[8,17408]{1,0:T(8,128)S(1)} %broadcast_select_fusion.5), channel_id=1, source_target_pairs={{0,128},{4,132},{8,136},{12,140},{16,144},{20,148},{24,152},{28,15... | collective-permute-start | bytes 1671176 | tf_op jit(solution)/shard_map/ppermute | solution.py:27
  135.7 77.4 %copy-start.15 = (pred[8]{0:T(512)(128)(4,1)S(1)}, pred[8]{0:T(512)(128)(4,1)}, u32[]{:S(2)}) copy-start(pred[8]{0:T(512)(128)(4,1)} %copy-done.14) | copy-start | bytes 28
  135.7 77.4 %copy-start.18 = (pred[8]{0:T(512)(128)(4,1)S(1)}, pred[8]{0:T(512)(128)(4,1)}, u32[]{:S(2)}) copy-start(pred[8]{0:T(512)(128)(4,1)} %get-tuple-element.86) | copy-start | bytes 28
  193.0 21.6 %copy-start.12 = (bf16[64,256]{1,0:T(8,128)(2,1)S(1)}, bf16[64,256]{1,0:T(8,128)(2,1)}, u32[]{:S(2)}) copy-start(bf16[64,256]{1,0:T(8,128)(2,1)} %param.37) | copy-start | bytes 98308
  193.1 21.6 %copy-start.27 = (f32[256]{0:T(256)S(1)}, f32[256]{0:T(256)}, u32[]{:S(2)}) copy-start(f32[256]{0:T(256)} %param.38) | copy-start | bytes 3076
  233.2 56.4 %copy-start.9 = (f32[2048]{0:T(1024)S(1)}, f32[2048]{0:T(1024)}, u32[]{:S(2)}) copy-start(f32[2048]{0:T(1024)} %param.31) | copy-start | bytes 24580
  233.2 56.6 %copy-start.10 = (f32[1,2048]{1,0:T(1,128)S(1)}, f32[1,2048]{1,0:T(1,128)}, u32[]{:S(2)}) copy-start(f32[1,2048]{1,0:T(1,128)} %get-tuple-element.99) | copy-start | bytes 24580
  237.8 82.5 %reduce-scatter.2.cloned.1.call-start = ((), (), s32[]{:S(2)}) async-start(), calls=%async_computation.2 | async-start | bytes 163840 | tf_op jit(solution)/shard_map/reduce_scatter | solution.py:302
  293.2 27.9 %copy-start.28 = (pred[8,4]{1,0:T(8,128)(4,1)S(1)}, pred[8,4]{1,0:T(8,128)(4,1)}, u32[]{:S(2)}) copy-start(pred[8,4]{1,0:T(8,128)(4,1)} %iota_compare_fusion.1) | copy-start | bytes 100
  (21 other events, 193.2 us)
Sparse Core Ops, SparseCore 0:
  237.9 50.3 all-reduce.2
  296.9 23.3 reduce-scatter.1
